TPU v7x, 128 devices: a whole 4x4x4 slice. The times are simulated.
128 devices in a mesh: req: 32 (over y, z, core), tp: 4 (over x).
Axes of the slice: x: 4, y: 4, z: 4, core: 2. Of those that a mesh axis runs over, the one named last changes fastest.
Arguments:
- states: bfloat16 [64, 512, 1024], P('req', 'tp'), may hold values from -45 to 45
- lengths: int32 [64], P('req'), may hold values from 3 to 512, as said below
- w_qkv: bfloat16 [1024, 3, 1024], P(None, None, 'tp'), may hold values from -0.1875 to 0.1875
- b_qkv: float32 [3, 1024], P(None, 'tp'), may hold values from -3 to 3
- w_out: bfloat16 [1024, 1024], P('tp'), may hold values from -0.1875 to 0.1875
- b_out: float32 [1024], replicated, may hold values from -3 to 3
- ln1_gain: float32 [1024], replicated, may hold values from 0.1 to 1.9
- ln1_shift: float32 [1024], replicated, may hold values from -3 to 3
- w_up: bfloat16 [1024, 4096], P(None, 'tp'), may hold values from -0.1875 to 0.1875
- b_up: float32 [4096], P('tp'), may hold values from -3 to 3
- w_down: bfloat16 [4096, 1024], P('tp'), may hold values from -0.09375 to 0.09375
- b_down: float32 [1024], replicated, may hold values from -3 to 3
- ln2_gain: float32 [1024], replicated, may hold values from 0.1 to 1.9
- ln2_shift: float32 [1024], replicated, may hold values from -3 to 3
- index_rows: bfloat16 [524288, 1024], P(('req', 'tp')), may hold values from -0.1875 to 0.1875
- cand_ids: int32 [64, 64], P('req', 'tp'), may hold values from 0 to 524287
Outputs:
- hidden_out: bfloat16 [64, 512, 1024], P('req', 'tp')
- scores: float32 [64, 64], P('req', 'tp')
Inputs may be any that keep to these rules, and one draw needn't show every extreme that they name: Valid positions are the first lengths ones of a text; in every draw some text has 512.
All inputs are finite; a program needn't handle non-finite values.
Results may differ from a plain program's by a relative error of at most 0.015.
Values may be sent and summed in bfloat16 or wider, within the bound.
A program may use at most 128 MiB of HBM per device.

v0:
```python
import jax
import jax.numpy as jnp
from jax import lax
from jax.sharding import PartitionSpec as P

HEAD_DIM = 64
WINDOW = 512
layer_eps = 1e-05
norm_eps = 1e-06


def layer_norm(values, gain, shift):
    centre = values - jnp.mean(values, axis=-1, keepdims=True)
    spread = jnp.mean(centre * centre, axis=-1, keepdims=True)
    return centre * lax.rsqrt(spread + layer_eps) * gain + shift


def window_attention(queries_h, keys_h, values_h, length):
    seq_len = queries_h.shape[0]
    half_window = WINDOW // 2
    padding = ((half_window, half_window), (0, 0), (0, 0))
    keys_padded = jnp.pad(keys_h, padding)
    values_padded = jnp.pad(values_h, padding)
    scale_factor = HEAD_DIM ** (-0.5)

    def one_block(block_idx):
        blk_start = block_idx * WINDOW
        query_pos = blk_start + jnp.arange(WINDOW, dtype=jnp.int32)
        key_pos = blk_start - half_window + jnp.arange(2 * WINDOW, dtype=jnp.int32)
        keep_mask = (
            (jnp.abs(query_pos[:, None] - key_pos[None, :]) <= half_window)
            & (key_pos[None, :] >= 0)
            & (key_pos[None, :] < length)
        )
        logits = (
            jnp.einsum("qhe,khe->hqk", queries_h, keys_padded, preferred_element_type=jnp.float32)
            * scale_factor
        )
        logits = jnp.where(keep_mask[None], logits, jnp.float32(-1e30))
        top_val = jnp.max(logits, axis=-1, keepdims=True)
        expo = jnp.exp(logits - top_val)
        attn_weights = (expo / jnp.sum(expo, axis=-1, keepdims=True)).astype(jnp.bfloat16)
        context = jnp.einsum(
            "hqk,khe->qhe", attn_weights, values_padded, preferred_element_type=jnp.float32
        )
        context = jnp.where((query_pos < length)[:, None, None], context, jnp.float32(0.0))
        return context.astype(jnp.bfloat16)

    blocks = lax.map(one_block, jnp.arange(seq_len // WINDOW, dtype=jnp.int32))
    return blocks.reshape(seq_len, queries_h.shape[1] * HEAD_DIM)


def per_device(
    states,
    lengths,
    w_qkv,
    b_qkv,
    w_out,
    b_out,
    ln1_gain,
    ln1_shift,
    w_up,
    b_up,
    w_down,
    b_down,
    ln2_gain,
    ln2_shift,
    index_rows,
    cand_ids,
):
    tp_count = lax.axis_size("tp")
    tp_rank = lax.axis_index("tp")
    req_count = lax.axis_size("req")
    text_count, row_share, model_width = states.shape
    full_states = lax.all_gather(states, "tp", axis=1, tiled=True)
    seq_len = full_states.shape[1]
    local_width = w_qkv.shape[2]
    heads_here = local_width // HEAD_DIM
    projected = (
        jnp.einsum("tsd,dce->tsce", full_states, w_qkv, preferred_element_type=jnp.float32) + b_qkv
    ).astype(jnp.bfloat16)
    queries_h = projected[:, :, 0].reshape(text_count, seq_len, heads_here, HEAD_DIM)
    keys_h = projected[:, :, 1].reshape(text_count, seq_len, heads_here, HEAD_DIM)
    values_h = projected[:, :, 2].reshape(text_count, seq_len, heads_here, HEAD_DIM)

    def per_text(bundle):
        return window_attention(bundle[0], bundle[1], bundle[2], bundle[3])

    context = lax.map(per_text, (queries_h, keys_h, values_h, lengths))
    partial_value = jnp.einsum("tsk,kd->tsd", context, w_out, preferred_element_type=jnp.float32)
    attn_sum = lax.psum(partial_value.astype(jnp.bfloat16), "tp").astype(jnp.float32)
    normed_full = layer_norm(
        full_states.astype(jnp.float32) + attn_sum + b_out, ln1_gain, ln1_shift
    ).astype(jnp.bfloat16)
    normed_local = lax.dynamic_slice_in_dim(normed_full, tp_rank * row_share, row_share, 1)
    up_act = jax.nn.gelu(
        jnp.einsum("tsd,df->tsf", normed_full, w_up, preferred_element_type=jnp.float32) + b_up,
        approximate=False,
    ).astype(jnp.bfloat16)
    down_part = jnp.einsum("tsf,fd->tsd", up_act, w_down, preferred_element_type=jnp.float32)
    down_sum = lax.psum_scatter(
        down_part.astype(jnp.bfloat16), "tp", scatter_dimension=1, tiled=True
    ).astype(jnp.float32)
    hidden_out = layer_norm(
        normed_local.astype(jnp.float32) + down_sum + b_down, ln2_gain, ln2_shift
    ).astype(jnp.bfloat16)
    positions = tp_rank * row_share + jnp.arange(row_share, dtype=jnp.int32)
    is_valid = positions[None, :] < lengths[:, None]
    local_pool = jnp.sum(
        jnp.where(is_valid[:, :, None], hidden_out.astype(jnp.float32), jnp.float32(0.0)), axis=1
    )
    pooled = lax.psum(local_pool, "tp") / lengths.astype(jnp.float32)[:, None]
    query_vec = (
        pooled * lax.rsqrt(jnp.mean(pooled * pooled, axis=-1, keepdims=True) + norm_eps)
    ).astype(jnp.bfloat16)
    all_queries = lax.all_gather(query_vec, "req", axis=0, tiled=True)
    quarter = cand_ids.shape[1]
    gathered_ids = lax.all_gather(cand_ids, ("req", "tp"), axis=0, tiled=True)
    all_ids = (
        gathered_ids.reshape(req_count, tp_count, text_count, quarter)
        .transpose(0, 2, 1, 3)
        .reshape(req_count * text_count, tp_count * quarter)
    )
    rows_here = index_rows.shape[0]
    first_row = (lax.axis_index("req") * tp_count + tp_rank) * rows_here
    local_ids = all_ids - first_row
    is_owned = (local_ids >= 0) & (local_ids < rows_here)
    safe_ids = jnp.clip(local_ids, 0, rows_here - 1)
    fetched = jnp.take(index_rows, safe_ids.reshape(-1), axis=0).reshape(
        safe_ids.shape[0], safe_ids.shape[1], model_width
    )
    picked = jnp.einsum("td,tcd->tc", all_queries, fetched, preferred_element_type=jnp.float32)
    owner_terms = jnp.where(is_owned, picked, jnp.float32(0.0))
    owner_terms = (
        owner_terms.reshape(req_count, text_count, tp_count, quarter)
        .transpose(0, 2, 1, 3)
        .reshape(req_count * tp_count * text_count, quarter)
    )
    scores = lax.psum_scatter(owner_terms, ("req", "tp"), scatter_dimension=0, tiled=True)
    return (hidden_out, scores)


def solution(mesh):
    placed = (
        P("req", "tp", None),
        P("req"),
        P(None, None, "tp"),
        P(None, "tp"),
        P("tp", None),
        P(),
        P(),
        P(),
        P(None, "tp"),
        P("tp"),
        P("tp", None),
        P(),
        P(),
        P(),
        P(("req", "tp"), None),
        P("req", "tp"),
    )
    return jax.shard_map(
        per_device,
        mesh=mesh,
        in_specs=placed,
        out_specs=(P("req", "tp", None), P("req", "tp")),
        check_vma=False,
    )
```

profile of v0, /device:TPU:1, one launch (start us, length us, event | category | flops | bytes accessed | tf_op | source)
XLA Modules:
  0.0 362.5 jit_solution(10841223569805811967)
XLA Ops:
  8.0 35.7 %all-gather.4.cloned.1.call-done = bf16[2,512,1024]{2,1,0:T(8,128)(2,1)} async-done(((bf16[2,128,1024]{2,1,0:T(8,128)(2,1)}), bf16[2,512,1024]{2,1,0:T(8,128)(2,1)}) %all-gather.4.cloned.1.call-update) | async-done | bytes 2097168 | tf_op jit(solution)/shard_map/all_gather | solution.py:75
  43.7 3.9 %add_convert_fusion.1 = bf16[2,512,3,256]{1,3,2,0:T(8,128)(2,1)S(1)} fusion(f32[3,256]{1,0:T(4,128)} %param.21, bf16[1024,3,256]{2,0,1:T(8,128)(2,1)} %param.20, bf16[2,512,1024]{2,1,0:T(8,128)(2,1)} %all-gather.4.cloned.1.call-done), kind=kOutput, calls=%fused_computation.68 | convolution fusion | flops 1612185600 | bytes 5245952 | tf_op jit(solution)/shard_map/tsd,dce->tsce/dot_general | solution.py:80
  47.6 1.2 fusion.150
  48.8 33.0 %while.17 = (s32[]{:T(128)}, bf16[2,512,256]{1,2,0:T(8,128)(2,1)}, s32[2]{0:T(128)S(1)}, bf16[2,512,4,64]{1,3,2,0:T(8,128)(2,1)}, bf16[2,512,4,64]{1,3,2,0:T(8,1...) while((s32[]{:T(128)}, bf16[2,512,256]{1,2,0:T(8,128)(2,1)}, s32[2]{0:T(128)S(1)}, ...), condition=%wide.region_3.4_spmd, body=%wide.region_0.3_spmd.sunk | while | flops 552343040 | bytes 24671904 | solution.py:89
  52.0 6.9 %fusion.166 = (f32[4,512]{1,0:T(4,128)S(1)}, f32[4,512,1024]{2,1,0:T(8,128)}) fusion(pred[512,1024]{1,0:T(8,128)(4,1)S(1)} %fusion.165, bf16[512,4,64]{0,2,1:T(8,128)(2,1)S(1)} %get-tuple-element.195, bf16[2,512,4,64]{1,3,2,0:T(8,128)(2,1)} %get-tuple-element.217, s32[]{:T(128)} %get-tuple-element.206), kind=kOutput, calls=%fused_computation.171.clone.1 | convolution fusion | flops 276825088 | bytes 9445888 | tf_op jit(solution)/shard_map/while/body/eval_jaxpr/while/body/eval_jaxpr/sub | solution.py:41
  59.6 4.9 %fusion.167 = bf16[4,64,512]{2,1,0:T(8,128)(2,1)S(1)} fusion(f32[4,512,1024]{2,1,0:T(8,128)} %get-tuple-element.196, f32[4,512]{1,0:T(4,128)S(1)} %get-tuple-element.197, bf16[512,4,64]{0,2,1:T(8,128)(2,1)S(1)} %get-tuple-element.198, pred[512]{0:T(512)(128)(4,1)S(1)} %iota_compare_fusion.2), kind=kOutput, calls=%fused_computation.14.clone.1 | convolution fusion | flops 272891904 | bytes 8921600 | tf_op jit(solution)/shard_map/while/body/eval_jaxpr/while/body/eval_jaxpr/hqk,khe->qhe/dot_general | solution.py:43
  67.4 1.1 dynamic-slice_bitcast_fusion.3
  68.5 6.9 %fusion.166 = (f32[4,512]{1,0:T(4,128)S(1)}, f32[4,512,1024]{2,1,0:T(8,128)}) fusion(pred[512,1024]{1,0:T(8,128)(4,1)S(1)} %fusion.165, bf16[512,4,64]{0,2,1:T(8,128)(2,1)S(1)} %get-tuple-element.195, bf16[2,512,4,64]{1,3,2,0:T(8,128)(2,1)} %get-tuple-element.217, s32[]{:T(128)} %get-tuple-element.206), kind=kOutput, calls=%fused_computation.171.clone.1 | convolution fusion | flops 276825088 | bytes 9445888 | tf_op jit(solution)/shard_map/while/body/eval_jaxpr/while/body/eval_jaxpr/sub | solution.py:41
  76.1 4.9 %fusion.167 = bf16[4,64,512]{2,1,0:T(8,128)(2,1)S(1)} fusion(f32[4,512,1024]{2,1,0:T(8,128)} %get-tuple-element.196, f32[4,512]{1,0:T(4,128)S(1)} %get-tuple-element.197, bf16[512,4,64]{0,2,1:T(8,128)(2,1)S(1)} %get-tuple-element.198, pred[512]{0:T(512)(128)(4,1)S(1)} %iota_compare_fusion.2), kind=kOutput, calls=%fused_computation.14.clone.1 | convolution fusion | flops 272891904 | bytes 8921600 | tf_op jit(solution)/shard_map/while/body/eval_jaxpr/while/body/eval_jaxpr/hqk,khe->qhe/dot_general | solution.py:43
  81.8 3.2 convolution_convert_fusion
  85.3 58.6 %all-reduce.5.cloned.1.call-done = bf16[2,512,1024]{2,1,0:T(8,128)(2,1)} async-done(((bf16[2,512,1024]{2,1,0:T(8,128)(2,1)}), bf16[2,512,1024]{2,1,0:T(8,128)(2,1)}) %all-reduce.5.cloned.1.call-update) | async-done | bytes 2097168 | tf_op jit(solution)/shard_map/psum | solution.py:91
  143.9 3.1 fusion.54
  148.5 1.2 add_convert_fusion
  149.8 3.4 fusion.103
  153.2 12.5 %fusion.92 = bf16[2,512,1024]{2,1,0:T(8,128)(2,1)} fusion(bf16[1024,1024]{1,0:T(8,128)(2,1)S(1)} %copy-done.13, f32[2,512,1024]{2,1,0:T(8,128)S(1)} %get-tuple-element.149, f32[1024]{0:T(1024)S(1)} %copy-done.14, u8[512,1024]{1,0:T(8,128)(4,1)S(1)} %get-tuple-element.123, u8[512,1024]{1,0:T(8,128)(4,1)S(1)} %get-tuple-element.122), kind=kOutput, calls=%fused_computation.105 | convolution fusion | flops 2222981120 | bytes 9441280 | tf_op jit(solution)/shard_map/tsf,fd->tsd/dot_general | solution.py:100
  165.7 55.1 %all-gather = s32[128,2,16]{2,1,0:T(2,128)S(1)} all-gather(s32[1,2,16]{2,1,0:T(2,128)S(1)} %bitcast.89), channel_id=1, replica_groups=mesh['req'=32,'tp'=4] {'req','tp'}, dimensions={0}, use_global_device_ids=true | all-gather | bytes 16512 | tf_op jit(solution)/shard_map/all_gather | solution.py:118
  221.7 25.4 %gather_fusion = bf16[4096,1024]{1,0:T(8,128)(2,1)} fusion(bf16[4096,1024]{1,0:T(8,128)(2,1)} %param.32, s32[4096]{0:T(1024)S(1)} %broadcast_clamp_fusion), kind=kCustom, calls=%fused_computation | custom fusion | bytes 16793600 | tf_op jit(solution)/shard_map/jit(_take)/gather | solution.py:129
  247.2 1.5 fusion.104
  248.6 1.5 multiply_reduce_fusion.1
  250.2 2.4 select_reduce_fusion
  252.6 8.4 %psum.15 = f32[2,1024]{1,0:T(2,128)S(1)} all-reduce(f32[2,1024]{1,0:T(2,128)S(1)} %get-tuple-element.138), channel_id=1, replica_groups=mesh['req'=32,'tp'=4] {'tp'}, use_global_device_ids=true, to_apply=%region_11.12 | all-reduce | flops 2048 | bytes 16384 | tf_op jit(solution)/shard_map/psum | solution.py:112
  261.3 25.0 %all-gather.1 = bf16[32,2,1024]{2,1,0:T(2,128)(2,1)S(1)} all-gather(bf16[1,2,1024]{2,1,0:T(2,128)(2,1)S(1)} %fusion.108), channel_id=1, replica_groups=mesh['req'=32,'tp'=4] {'req'}, dimensions={0}, use_global_device_ids=true | all-gather | bytes 135168 | tf_op jit(solution)/shard_map/all_gather | solution.py:116
  286.4 4.7 %fusion.41 = f32[64,1,64]{2,1,0:T(1,128)S(1)} fusion(bf16[64,1024,1]{1,2,0:T(2,128)(2,1)S(1)} %reshape.275, bf16[64,64,1024]{2,1,0:T(8,128)(2,1)} %bitcast.75, pred[64,64]{1,0:T(8,128)(4,1)S(1)} %compare_and_fusion.1), kind=kOutput, calls=%fused_computation.38 | convolution fusion | flops 12582912 | bytes 8540160 | tf_op jit(solution)/shard_map/td,tcd->tc/dot_general | solution.py:132
  291.4 64.0 %all-reduce.2 = f32[256,16]{1,0:T(8,128)S(1)} all-reduce(f32[256,16]{1,0:T(8,128)S(1)} %bitcast.82), channel_id=3, replica_groups=mesh['req'=32,'tp'=4] {'req','tp'}, use_global_device_ids=true, to_apply=%region_13.14.clone | all-reduce | flops 4096 | bytes 32768
  (83 shorter events, 12.6 us)
Async XLA Ops:
  7.2 142.6 %copy-start = (bf16[1024,1024]{1,0:T(8,128)(2,1)S(1)}, bf16[1024,1024]{1,0:T(8,128)(2,1)}, u32[]{:S(2)}) copy-start(bf16[1024,1024]{1,0:T(8,128)(2,1)} %param.26) | copy-start | bytes 6291460
  7.2 36.5 %all-gather.4.cloned.1.call-start = ((), (), s32[]{:S(2)}) async-start(), calls=%async_computation.1 | async-start | bytes 2621440 | tf_op jit(solution)/shard_map/all_gather | solution.py:75
  7.9 136.0 %all-reduce.5.cloned.1.call-start = ((), (), s32[]{:S(2)}) async-start(), calls=%async_computation.2 | async-start | bytes 4194304 | tf_op jit(solution)/shard_map/psum | solution.py:91
  8.0 40.8 %copy-start.15 = (s32[2]{0:T(128)S(1)}, s32[2]{0:T(128)}, u32[]{:S(2)}) copy-start(s32[2]{0:T(128)} %param.19) | copy-start | bytes 28
  59.6 4.9 %copy-start.4 = (bf16[2,512,256]{1,2,0:T(8,128)(2,1)S(1)}, bf16[2,512,256]{1,2,0:T(8,128)(2,1)}, u32[]{:S(2)}) copy-start(bf16[2,512,256]{1,2,0:T(8,128)(2,1)} %get-tuple-element.207) | copy-start | bytes 1572868 | tf_op jit(solution)/shard_map/while
  64.5 0.8 copy-start.5
  76.0 4.9 %copy-start.4 = (bf16[2,512,256]{1,2,0:T(8,128)(2,1)S(1)}, bf16[2,512,256]{1,2,0:T(8,128)(2,1)}, u32[]{:S(2)}) copy-start(bf16[2,512,256]{1,2,0:T(8,128)(2,1)} %get-tuple-element.207) | copy-start | bytes 1572868 | tf_op jit(solution)/shard_map/while
  81.0 0.8 copy-start.5
  81.8 62.1 %copy-start.7 = (f32[1024]{0:T(1024)S(1)}, f32[1024]{0:T(1024)}, u32[]{:S(2)}) copy-start(f32[1024]{0:T(1024)} %param.23) | copy-start | bytes 12292
  85.1 63.4 %copy-start.10 = (f32[1024]{0:T(1024)S(1)}, f32[1024]{0:T(1024)}, u32[]{:S(2)}) copy-start(f32[1024]{0:T(1024)} %param.25) | copy-start | bytes 12292
  85.1 63.4 %copy-start.11 = (f32[1024]{0:T(1024)S(1)}, f32[1024]{0:T(1024)}, u32[]{:S(2)}) copy-start(f32[1024]{0:T(1024)} %param.24) | copy-start | bytes 12292
  85.1 162.1 %reduce-scatter.2.cloned.1.call-start = ((), (), s32[]{:S(2)}) async-start(), calls=%async_computation.3 | async-start | bytes 2621440 | tf_op jit(solution)/shard_map/reduce_scatter | solution.py:101
  143.9 3.1 copy-start.1
  143.9 3.5 copy-start.2
  148.4 1.3 copy-start.14
  149.8 3.4 copy-start.3
  149.8 3.4 copy-start.13
  153.2 12.5 %copy-start.12 = (s32[2,16]{1,0:T(2,128)S(1)}, s32[2,16]{1,0:T(2,128)}, u32[]{:S(2)}) copy-start(s32[2,16]{1,0:T(2,128)} %param.33) | copy-start | bytes 388
  221.6 25.5 %copy-start.6 = (f32[1024]{0:T(1024)S(1)}, f32[1024]{0:T(1024)}, u32[]{:S(2)}) copy-start(f32[1024]{0:T(1024)} %param.29) | copy-start | bytes 12292
  221.7 28.5 %copy-start.8 = (f32[1024]{0:T(1024)S(1)}, f32[1024]{0:T(1024)}, u32[]{:S(2)}) copy-start(f32[1024]{0:T(1024)} %param.31) | copy-start | bytes 12292
  221.7 28.5 %copy-start.9 = (f32[1024]{0:T(1024)S(1)}, f32[1024]{0:T(1024)}, u32[]{:S(2)}) copy-start(f32[1024]{0:T(1024)} %param.30) | copy-start | bytes 12292
Sparse Core Ops, SparseCore 0:
  9.7 34.0 all-gather.3
  85.2 58.6 all-reduce.4
  165.8 29.5 reduce-scatter.1
where the time goes:
time: 363 us
  blocking collectives  153 us (42%)
  waiting for transfers between devices  95 us (26%)
  matrix products  51.4 us (14%)
  local copies, waits for them, and re-layouts  33.3 us (9%)
  other arithmetic  15.6 us (4%)
  between operations  14.1 us (4%)
    unnamed x1, blocking collectives  64 us
    psum x1, waiting for transfers between devices, per_device(): lax.psum(partial_value.astype(jnp.bfloat16), 'tp').astype(jnp.float32)  58.6 us
    all_gather x1, blocking collectives, per_device(): gathered_ids = lax.all_gather(cand_ids, ('req', 'tp'), axis=0, tiled=True)  55.1 us
    all_gather x1, waiting for transfers between devices, per_device(): full_states = lax.all_gather(states, 'tp', axis=1, tiled=True)  35.7 us
    gather x1, local copies, waits for them, and re-layouts, per_device(): jnp.take(index_rows, safe_ids.reshape(-1), axis=0)  25.4 us
    all_gather x1, blocking collectives, per_device(): all_queries = lax.all_gather(query_vec, 'req', axis=0, tiled=True)  25 us
    sub x2, matrix products, one_block(): expo = jnp.exp(logits - top_val)  13.8 us
    dot_general x1, matrix products, per_device(): jnp.einsum('tsf,fd->tsd', up_act, w_down, preferred_element_type=jnp.floa...  12.5 us
  transfers between devices with their start and end apart: 3, of which 2 were waited for; matrix products, arithmetic and copies ran while one was open for 7% of the time, Pallas kernels for 0%

commit v1 on v0

--- a/solution.py
+++ b/solution.py
@@ -7,6 +7,11 @@
 WINDOW = 512
 layer_eps = 1e-05
 norm_eps = 1e-06
+
+
+def summed_here(x, axis):
+    pieces = lax.all_gather(x, axis)
+    return jnp.sum(pieces, axis=0)
 
 
 def layer_norm(values, gain, shift):
@@ -88,7 +93,7 @@
 
     context = lax.map(per_text, (queries_h, keys_h, values_h, lengths))
     partial_value = jnp.einsum("tsk,kd->tsd", context, w_out, preferred_element_type=jnp.float32)
-    attn_sum = lax.psum(partial_value.astype(jnp.bfloat16), "tp").astype(jnp.float32)
+    attn_sum = summed_here(partial_value.astype(jnp.bfloat16), "tp").astype(jnp.float32)
     normed_full = layer_norm(
         full_states.astype(jnp.float32) + attn_sum + b_out, ln1_gain, ln1_shift
     ).astype(jnp.bfloat16)

time: 363 us -> 395 us (1.088)
  waiting for transfers between devices: 95 us -> 120 us
  other arithmetic: 15.6 us -> 23 us
    all_gather x0 -> x1, waiting for transfers between devices: none -> 83.1 us  [summed_here(): pieces = lax.all_gather(x, axis)]
    psum x1 -> x0, waiting for transfers between devices: 58.6 us -> none  [per_device(): lax.psum(partial_value.astype(jnp.bfloat16), 'tp').astype(jnp.float32)]
    reduce_sum x0 -> x1, other arithmetic: none -> 7.42 us  [summed_here(): return jnp.sum(pieces, axis=0)]
where the time goes in v1:
time: 395 us
  blocking collectives  153 us (39%)
  waiting for transfers between devices  120 us (30%)
  matrix products  51.3 us (13%)
  local copies, waits for them, and re-layouts  33.3 us (8%)
  other arithmetic  23 us (6%)
  between operations  14.1 us (4%)
    all_gather x1, waiting for transfers between devices, summed_here(): pieces = lax.all_gather(x, axis)  83.1 us
    unnamed x1, blocking collectives  63.8 us
    all_gather x1, blocking collectives, per_device(): gathered_ids = lax.all_gather(cand_ids, ('req', 'tp'), axis=0, tiled=True)  56 us
    all_gather x1, waiting for transfers between devices, per_device(): full_states = lax.all_gather(states, 'tp', axis=1, tiled=True)  35.7 us
    all_gather x1, blocking collectives, per_device(): all_queries = lax.all_gather(query_vec, 'req', axis=0, tiled=True)  25.7 us
    gather x1, local copies, waits for them, and re-layouts, per_device(): jnp.take(index_rows, safe_ids.reshape(-1), axis=0)  25.4 us
    sub x2, matrix products, one_block(): expo = jnp.exp(logits - top_val)  13.8 us
    dot_general x1, matrix products, per_device(): jnp.einsum('tsf,fd->tsd', up_act, w_down, preferred_element_type=jnp.floa...  12.5 us
  transfers between devices with their start and end apart: 3, of which 2 were waited for; matrix products, arithmetic and copies ran while one was open for 7% of the time, Pallas kernels for 0%

profile of v1, /device:TPU:1, one launch (start us, length us, event | category | flops | bytes accessed | tf_op | source)
XLA Modules:
  0.0 394.6 jit_solution(3761492354183344975)
XLA Ops:
  8.0 35.7 %all-gather.6.cloned.1.call-done = bf16[2,512,1024]{2,1,0:T(8,128)(2,1)} async-done(((bf16[2,128,1024]{2,1,0:T(8,128)(2,1)}), bf16[2,512,1024]{2,1,0:T(8,128)(2,1)}) %all-gather.6.cloned.1.call-update) | async-done | bytes 2097168 | tf_op jit(solution)/shard_map/all_gather | solution.py:80
  43.7 3.9 add_convert_fusion.1
  47.6 1.2 fusion.150
  48.8 33.0 %while.17 = (s32[]{:T(128)}, bf16[2,512,256]{1,2,0:T(8,128)(2,1)}, s32[2]{0:T(128)S(1)}, bf16[2,512,4,64]{1,3,2,0:T(8,128)(2,1)}, bf16[2,512,4,64]{1,3,2,0:T(8,1...) while((s32[]{:T(128)}, bf16[2,512,256]{1,2,0:T(8,128)(2,1)}, s32[2]{0:T(128)S(1)}, ...), condition=%wide.region_3.4_spmd, body=%wide.region_0.3_spmd.sunk | while | flops 552343040 | bytes 24671904 | solution.py:94
  52.0 6.9 %fusion.166 = (f32[4,512]{1,0:T(4,128)S(1)}, f32[4,512,1024]{2,1,0:T(8,128)}) fusion(pred[512,1024]{1,0:T(8,128)(4,1)S(1)} %fusion.165, bf16[512,4,64]{0,2,1:T(8,128)(2,1)S(1)} %get-tuple-element.195, bf16[2,512,4,64]{1,3,2,0:T(8,128)(2,1)} %get-tuple-element.217, s32[]{:T(128)} %get-tuple-element.206), kind=kOutput, calls=%fused_computation.171.clone.1 | convolution fusion | flops 276825088 | bytes 9445888 | tf_op jit(solution)/shard_map/while/body/eval_jaxpr/while/body/eval_jaxpr/sub | solution.py:46
  59.6 4.9 %fusion.167 = bf16[4,64,512]{2,1,0:T(8,128)(2,1)S(1)} fusion(f32[4,512,1024]{2,1,0:T(8,128)} %get-tuple-element.196, f32[4,512]{1,0:T(4,128)S(1)} %get-tuple-element.197, bf16[512,4,64]{0,2,1:T(8,128)(2,1)S(1)} %get-tuple-element.198, pred[512]{0:T(512)(128)(4,1)S(1)} %iota_compare_fusion.2), kind=kOutput, calls=%fused_computation.14.clone.1 | convolution fusion | flops 272891904 | bytes 8921600 | tf_op jit(solution)/shard_map/while/body/eval_jaxpr/while/body/eval_jaxpr/hqk,khe->qhe/dot_general | solution.py:48
  68.5 6.9 %fusion.166 = (f32[4,512]{1,0:T(4,128)S(1)}, f32[4,512,1024]{2,1,0:T(8,128)}) fusion(pred[512,1024]{1,0:T(8,128)(4,1)S(1)} %fusion.165, bf16[512,4,64]{0,2,1:T(8,128)(2,1)S(1)} %get-tuple-element.195, bf16[2,512,4,64]{1,3,2,0:T(8,128)(2,1)} %get-tuple-element.217, s32[]{:T(128)} %get-tuple-element.206), kind=kOutput, calls=%fused_computation.171.clone.1 | convolution fusion | flops 276825088 | bytes 9445888 | tf_op jit(solution)/shard_map/while/body/eval_jaxpr/while/body/eval_jaxpr/sub | solution.py:46
  76.1 4.9 %fusion.167 = bf16[4,64,512]{2,1,0:T(8,128)(2,1)S(1)} fusion(f32[4,512,1024]{2,1,0:T(8,128)} %get-tuple-element.196, f32[4,512]{1,0:T(4,128)S(1)} %get-tuple-element.197, bf16[512,4,64]{0,2,1:T(8,128)(2,1)S(1)} %get-tuple-element.198, pred[512]{0:T(512)(128)(4,1)S(1)} %iota_compare_fusion.2), kind=kOutput, calls=%fused_computation.14.clone.1 | convolution fusion | flops 272891904 | bytes 8921600 | tf_op jit(solution)/shard_map/while/body/eval_jaxpr/while/body/eval_jaxpr/hqk,khe->qhe/dot_general | solution.py:48
  81.8 3.2 convolution_convert_fusion
  85.3 83.1 %all-gather.8.cloned.1.call-done = bf16[8,512,1024]{2,1,0:T(8,128)(2,1)} async-done(((bf16[2,512,1024]{2,1,0:T(8,128)(2,1)}), bf16[8,512,1024]{2,1,0:T(8,128)(2,1)}) %all-gather.8.cloned.1.call-update) | async-done | bytes 8388624 | tf_op jit(solution)/shard_map/all_gather | solution.py:13
  168.4 7.4 %reduce_sum.80 = bf16[2,512,1024]{2,1,0:T(8,128)(2,1)} reduce(bf16[4,2,512,1024]{3,2,1,0:T(8,128)(2,1)} %bitcast.77, bf16[]{:T(256)} %constant.156.clone.1), dimensions={0}, to_apply=%region_4.5 | reduce | flops 3145728 | bytes 10485762 | tf_op jit(solution)/shard_map/reduce_sum | solution.py:14
  175.8 3.1 fusion.54
  180.4 1.2 add_convert_fusion
  181.7 3.4 fusion.103
  185.1 12.5 %fusion.92 = bf16[2,512,1024]{2,1,0:T(8,128)(2,1)} fusion(bf16[1024,1024]{1,0:T(8,128)(2,1)S(1)} %copy-done.13, f32[2,512,1024]{2,1,0:T(8,128)S(1)} %get-tuple-element.149, f32[1024]{0:T(1024)S(1)} %copy-done.14, u8[512,1024]{1,0:T(8,128)(4,1)S(1)} %get-tuple-element.123, u8[512,1024]{1,0:T(8,128)(4,1)S(1)} %get-tuple-element.122), kind=kOutput, calls=%fused_computation.105 | convolution fusion | flops 2222981120 | bytes 9441280 | tf_op jit(solution)/shard_map/tsf,fd->tsd/dot_general | solution.py:105
  197.6 56.0 %all-gather.1 = s32[128,2,16]{2,1,0:T(2,128)S(1)} all-gather(s32[1,2,16]{2,1,0:T(2,128)S(1)} %bitcast.91), channel_id=1, replica_groups=mesh['req'=32,'tp'=4] {'req','tp'}, dimensions={0}, use_global_device_ids=true | all-gather | bytes 16512 | tf_op jit(solution)/shard_map/all_gather | solution.py:123
  254.4 25.4 %gather_fusion = bf16[4096,1024]{1,0:T(8,128)(2,1)} fusion(bf16[4096,1024]{1,0:T(8,128)(2,1)} %param.32, s32[4096]{0:T(1024)S(1)} %broadcast_clamp_fusion), kind=kCustom, calls=%fused_computation | custom fusion | bytes 16793600 | tf_op jit(solution)/shard_map/jit(_take)/gather | solution.py:134
  279.9 1.5 fusion.104
  281.4 1.5 multiply_reduce_fusion.1
  283.0 2.4 select_reduce_fusion
  285.4 7.4 %psum.7 = f32[2,1024]{1,0:T(2,128)S(1)} all-reduce(f32[2,1024]{1,0:T(2,128)S(1)} %get-tuple-element.138), channel_id=1, replica_groups=mesh['req'=32,'tp'=4] {'tp'}, use_global_device_ids=true, to_apply=%region_11.12 | all-reduce | flops 2048 | bytes 16384 | tf_op jit(solution)/shard_map/psum | solution.py:117
  293.0 25.7 %all-gather.2 = bf16[32,2,1024]{2,1,0:T(2,128)(2,1)S(1)} all-gather(bf16[1,2,1024]{2,1,0:T(2,128)(2,1)S(1)} %fusion.108), channel_id=1, replica_groups=mesh['req'=32,'tp'=4] {'req'}, dimensions={0}, use_global_device_ids=true | all-gather | bytes 135168 | tf_op jit(solution)/shard_map/all_gather | solution.py:121
  318.8 4.7 %fusion.41 = f32[64,1,64]{2,1,0:T(1,128)S(1)} fusion(bf16[64,1024,1]{1,2,0:T(2,128)(2,1)S(1)} %reshape.276, bf16[64,64,1024]{2,1,0:T(8,128)(2,1)} %bitcast.76, pred[64,64]{1,0:T(8,128)(4,1)S(1)} %compare_and_fusion.1), kind=kOutput, calls=%fused_computation.38 | convolution fusion | flops 12582912 | bytes 8540160 | tf_op jit(solution)/shard_map/td,tcd->tc/dot_general | solution.py:137
  323.7 63.8 %all-reduce.2 = f32[256,16]{1,0:T(8,128)S(1)} all-reduce(f32[256,16]{1,0:T(8,128)S(1)} %bitcast.84), channel_id=4, replica_groups=mesh['req'=32,'tp'=4] {'req','tp'}, use_global_device_ids=true, to_apply=%region_13.14.clone | all-reduce | flops 4096 | bytes 32768
  (84 shorter events, 13.7 us)
Async XLA Ops:
  7.2 174.4 %copy-start = (bf16[1024,1024]{1,0:T(8,128)(2,1)S(1)}, bf16[1024,1024]{1,0:T(8,128)(2,1)}, u32[]{:S(2)}) copy-start(bf16[1024,1024]{1,0:T(8,128)(2,1)} %param.26) | copy-start | bytes 6291460
  7.2 36.5 %all-gather.6.cloned.1.call-start = ((), (), s32[]{:S(2)}) async-start(), calls=%async_computation.1 | async-start | bytes 2621440 | tf_op jit(solution)/shard_map/all_gather | solution.py:80
  7.9 160.4 %all-gather.8.cloned.1.call-start = ((), (), s32[]{:S(2)}) async-start(), calls=%async_computation.3 | async-start | bytes 10485760 | tf_op jit(solution)/shard_map/all_gather | solution.py:13
  8.0 40.8 %copy-start.15 = (s32[2]{0:T(128)S(1)}, s32[2]{0:T(128)}, u32[]{:S(2)}) copy-start(s32[2]{0:T(128)} %param.19) | copy-start | bytes 28
  59.6 4.9 %copy-start.4 = (bf16[2,512,256]{1,2,0:T(8,128)(2,1)S(1)}, bf16[2,512,256]{1,2,0:T(8,128)(2,1)}, u32[]{:S(2)}) copy-start(bf16[2,512,256]{1,2,0:T(8,128)(2,1)} %get-tuple-element.207) | copy-start | bytes 1572868 | tf_op jit(solution)/shard_map/while
  64.5 0.8 copy-start.5
  76.0 4.9 %copy-start.4 = (bf16[2,512,256]{1,2,0:T(8,128)(2,1)S(1)}, bf16[2,512,256]{1,2,0:T(8,128)(2,1)}, u32[]{:S(2)}) copy-start(bf16[2,512,256]{1,2,0:T(8,128)(2,1)} %get-tuple-element.207) | copy-start | bytes 1572868 | tf_op jit(solution)/shard_map/while
  81.0 0.8 copy-start.5
  85.1 194.8 %reduce-scatter.2.cloned.1.call-start = ((), (), s32[]{:S(2)}) async-start(), calls=%async_computation.2 | async-start | bytes 2621440 | tf_op jit(solution)/shard_map/reduce_scatter | solution.py:106
  168.4 7.4 %copy-start.7 = (f32[1024]{0:T(1024)S(1)}, f32[1024]{0:T(1024)}, u32[]{:S(2)}) copy-start(f32[1024]{0:T(1024)} %param.23) | copy-start | bytes 12292
  175.8 3.2 copy-start.1
  175.8 3.5 copy-start.2
  175.8 4.6 %copy-start.10 = (f32[1024]{0:T(1024)S(1)}, f32[1024]{0:T(1024)}, u32[]{:S(2)}) copy-start(f32[1024]{0:T(1024)} %param.25) | copy-start | bytes 12292
  175.8 4.6 %copy-start.11 = (f32[1024]{0:T(1024)S(1)}, f32[1024]{0:T(1024)}, u32[]{:S(2)}) copy-start(f32[1024]{0:T(1024)} %param.24) | copy-start | bytes 12292
  180.3 1.3 copy-start.14
  181.6 3.4 copy-start.3
  181.6 3.4 copy-start.13
  185.1 12.5 %copy-start.12 = (s32[2,16]{1,0:T(2,128)S(1)}, s32[2,16]{1,0:T(2,128)}, u32[]{:S(2)}) copy-start(s32[2,16]{1,0:T(2,128)} %param.33) | copy-start | bytes 388
  254.4 25.5 %copy-start.6 = (f32[1024]{0:T(1024)S(1)}, f32[1024]{0:T(1024)}, u32[]{:S(2)}) copy-start(f32[1024]{0:T(1024)} %param.29) | copy-start | bytes 12292
  254.4 28.5 %copy-start.8 = (f32[1024]{0:T(1024)S(1)}, f32[1024]{0:T(1024)}, u32[]{:S(2)}) copy-start(f32[1024]{0:T(1024)} %param.31) | copy-start | bytes 12292
  254.4 28.5 %copy-start.9 = (f32[1024]{0:T(1024)S(1)}, f32[1024]{0:T(1024)}, u32[]{:S(2)}) copy-start(f32[1024]{0:T(1024)} %param.30) | copy-start | bytes 12292
Sparse Core Ops, SparseCore 0:
  9.7 34.0 all-gather.5
  85.2 83.1 all-gather.7
  197.7 30.7 reduce-scatter.1
